TPU v7x, 256 devices: a whole 4x4x8 slice. The times are simulated.
256 devices in a mesh: tm: 4 (over z_lo), elem: 64 (over z_hi, x, y, core).
Axes of the slice: x: 4, y: 4, z: 8 (z_hi: 2, z_lo: 4; z = z_hi * 4 + z_lo), core: 2. Of those that a mesh axis runs over, the one named last changes fastest.
Arguments:
- state: float32 [16, 5, 64, 125, 128], P('tm', None, 'elem'), may hold values from -6 to 6
- metric_scale: float32 [64, 125, 128], P('elem'), may hold values from 0.1 to 0.4
- flux_jacobians: float32 [3, 5, 5], replicated, may hold values from -1.5 to 1.5, as said below
- preconditioner: float32 [16, 5, 5, 64, 128], P('tm', None, None, 'elem'), may hold values from -0.04 to 0.24
- inflow: float32 [16, 5, 64, 25], P('tm', None, 'elem'), may hold values from -6 to 6
Outputs:
- new_state: float32 [16, 5, 64, 125, 128], P('tm', None, 'elem')
- final_residual: float32 [16, 5, 64, 125, 128], P('tm', None, 'elem')
Inputs may be any that keep to these rules, and one draw needn't show every extreme that they name: `flux_jacobians`: symmetric in its last two dimensions.
All inputs are finite; a program needn't handle non-finite values.
Results may differ from a plain program's by a relative error of at most 0.0001.
Values sent between devices are 32-bit elements; how exact they have to be, the bound alone decides.
A program may use at most 128 MiB of HBM per device.

v0:
```python
import functools
import math

import jax
import jax.numpy as jnp
import numpy as np
from jax import lax
from jax.experimental import pallas as pl
from jax.experimental.pallas import tpu as pltpu
from jax.sharding import PartitionSpec as P

NI = 16
NV = 5
PR = 8
PASSES = 3
ROWS = 128
NODES = 125
FACE = 25
CHUNK = 32
MESH = pl.DeviceIdType.MESH
F32 = jnp.float32
BF16 = jnp.bfloat16


def gll_derivative():
    points = np.array([-1.0, -math.sqrt(3.0 / 7.0), 0.0, math.sqrt(3.0 / 7.0), 1.0])
    legendre = (35.0 * points**4 - 30.0 * points**2 + 3.0) / 8.0
    identity = np.eye(5, dtype=bool)
    spacing = np.where(identity, 1.0, points[:, None] - points[None, :])
    matrix = legendre[:, None] / legendre[None, :] / spacing
    corner = np.array([-5.0, 0.0, 0.0, 0.0, 5.0])[None, :]
    return np.where(identity, corner, matrix)


def coupling(offset):
    if offset % NI == 0:
        return 0.0
    angle = math.pi * offset / NI
    return 0.5 * (1.0 - 2.0 * (offset % 2)) * math.cos(angle) / math.sin(angle)


def patterns():
    table = gll_derivative()
    node = np.arange(NODES)
    index = [node // 25, (node // 5) % 5, node % 5]
    out = np.zeros((12, ROWS, ROWS))
    for d in range(3):
        others = [index[o] for o in range(3) if o != d]
        same = np.ones((NODES, NODES), bool)
        for o in others:
            same &= o[:, None] == o[None, :]
        out[d, :NODES, :NODES] = np.where(same, table[index[d][:, None], index[d][None, :]], 0.0)
        high, low = index[d] == 4, index[d] == 0
        out[d, node, node] += np.where(high, -5.0, 0.0) + np.where(low, 5.0, 0.0)
        out[3 + d, node, node] = np.where(high | low, 5.0, 0.0)
        for side, face in enumerate((high, low)):
            dest = node[face]
            for v in range(NV):
                out[6 + 2 * d + side, dest, FACE * v + np.arange(FACE)] = 5.0
    return out.astype(np.float32)


def split(value):
    high = value.astype(BF16)
    low = (value - high.astype(F32)).astype(BF16)
    return high, low


def kernel(
    state_ref, metric_ref, jac_ref, pre_ref, inflow_ref, pat_ref, new_ref, res_ref,
    us, u, spec, metric, inflow_cols, k_loc, k_tr, x_hi, x_lo, t_hi, t_lo, r, ax,
    stage, faces, raw, cross_out, cross_in, edge_out, edge_in,
    face_s, face_r, raw_s, raw_r, cross_s, cross_r, edge_s, edge_r,
):
    t = lax.axis_index("tm")
    e = lax.axis_index("elem")
    inner = jnp.logical_or(t == 1, t == 2)
    outer = jnp.logical_not(inner)
    ahead = t < 2
    beside = jnp.where(inner, jnp.where(t == 1, 0, 3), jnp.where(t == 0, 1, 2))
    opposite = jnp.where(inner, 3 - t, t)
    at_top = lax.rem(e, PR) == PR // 2 - 1
    at_bottom = lax.rem(e, PR) == PR // 2
    following = lax.rem(e + PR, 64)
    preceding = lax.rem(e + 64 - PR, 64)
    above = lax.rem(e + 1, 64)
    below = lax.rem(e + 63, 64)

    barrier = pltpu.get_barrier_semaphore()
    for peer in (following, preceding, above, below):
        pl.semaphore_signal(barrier, inc=1, device_id=(t, peer), device_id_type=MESH)
    for step in (1, 3):
        pl.semaphore_signal(barrier, inc=1, device_id=(lax.rem(t + step, 4), e), device_id_type=MESH)

    def face_copy(x, p, f):
        peer = (preceding, following, below, above)[f]
        return pltpu.make_async_remote_copy(
            src_ref=stage.at[x, p, f], dst_ref=faces.at[x, p, f],
            send_sem=face_s.at[x, p, f], recv_sem=face_r.at[x, p, f],
            device_id=(t, peer), device_id_type=MESH,
        )

    def raw_copy(v):
        return pltpu.make_async_remote_copy(
            src_ref=us.at[v], dst_ref=raw.at[v], send_sem=raw_s.at[v], recv_sem=raw_r.at[v],
            device_id=(beside, e), device_id_type=MESH,
        )

    def cross_copy(p, v):
        return pltpu.make_async_remote_copy(
            src_ref=cross_out.at[p, v], dst_ref=cross_in.at[p, v],
            send_sem=cross_s.at[p, v], recv_sem=cross_r.at[p, v],
            device_id=(opposite, e), device_id_type=MESH,
        )

    def edge_copy(p, v):
        return pltpu.make_async_remote_copy(
            src_ref=edge_out.at[p, v], dst_ref=edge_in.at[p, v],
            send_sem=edge_s.at[p, v], recv_sem=edge_r.at[p, v],
            device_id=(beside, e), device_id_type=MESH,
        )

    tail = pl.ds(ROWS - 8, 8)
    metric[tail, :] = jnp.zeros((8, 128), F32)
    metric[pl.ds(0, NODES), :] = metric_ref[...]
    for v in range(NV):
        for n in range(4):
            us[v, n, tail, :] = jnp.zeros((8, 128), F32)
            us[v, n, pl.ds(0, NODES), :] = state_ref[n, v]
    ax[:, tail, :] = jnp.zeros((2, 8, 128), F32)

    def clear(i, c):
        for x in range(PASSES + 1):
            for f in range(4):
                stage[x, i // 2, f, lax.rem(i, 2), tail, :] = jnp.zeros((8, 128), F32)
        return c

    lax.fori_loop(0, 4, clear, 0)

    def extract(source, x, p):
        def one(i, c):
            n = 2 * p + i
            for v in range(NV):
                rows = pl.ds(FACE * v, FACE)
                stage[x, p, 0, i, rows, :] = source[v, n, pl.ds(0, FACE), :]
                stage[x, p, 1, i, rows, :] = source[v, n, pl.ds(100, FACE), :]
                for k in range(5):
                    stage[x, p, 2, i, pl.ds(FACE * v + 5 * k, 5), :] = source[v, n, pl.ds(25 * k, 5), :]
                    stage[x, p, 3, i, pl.ds(FACE * v + 5 * k, 5), :] = source[v, n, pl.ds(25 * k + 20, 5), :]
            return c

        lax.fori_loop(0, 2, one, 0)

    def send_faces(x, p):
        face_copy(x, p, 0).start()
        face_copy(x, p, 1).start()

        @pl.when(jnp.logical_not(at_bottom))
        def _():
            face_copy(x, p, 2).start()

        @pl.when(jnp.logical_not(at_top))
        def _():
            face_copy(x, p, 3).start()

    for p in range(2):
        extract(us, 0, p)

    pl.semaphore_wait(barrier, 6)

    @pl.when(outer)
    def _():
        for v in range(NV):
            raw_copy(v).start()

    for p in range(2):
        send_faces(0, p)

    diagonal = lax.broadcasted_iota(jnp.int32, (FACE, FACE), 0) == lax.broadcasted_iota(
        jnp.int32, (FACE, FACE), 1
    )
    for n in range(4):
        for v in range(NV):
            row = inflow_ref[n, pl.ds(v, 1), :]
            column = jnp.sum(jnp.where(diagonal, row, 0.0), axis=1, keepdims=True)
            inflow_cols[v, n, pl.ds(0, FACE), :] = jnp.broadcast_to(column, (FACE, 128))

    damping = []
    for d in range(3):
        sums = []
        for v in range(NV):
            total = jnp.abs(jac_ref[d, v, 0])
            for w in range(1, NV):
                total = total + jnp.abs(jac_ref[d, v, w])
            sums.append(total)
        largest = sums[0]
        for v in range(1, NV):
            largest = jnp.maximum(largest, sums[v])
        damping.append(largest)
    var_of = lax.broadcasted_iota(jnp.int32, (1, 128), 1) // FACE
    for v in range(NV):
        rows = pl.ds(ROWS * v, ROWS)
        low_rows = pl.ds(ROWS * (NV + v), ROWS)
        for w in range(NV):
            block = jac_ref[0, v, w] * pat_ref[0]
            for d in range(1, 3):
                block = block + jac_ref[d, v, w] * pat_ref[d]
            if v == w:
                for d in range(3):
                    block = block + damping[d] * pat_ref[3 + d]
            hi, lo = split(block)
            k_loc[rows, ROWS * w : ROWS * (w + 1)] = hi
            k_loc[low_rows, ROWS * w : ROWS * (w + 1)] = lo
        for f in range(6):
            d, side = f // 2, f % 2
            coef = jnp.zeros((1, 128), F32)
            for w in range(NV):
                value = jac_ref[d, v, w]
                if side == 0:
                    value = value - damping[d] if v == w else value
                else:
                    value = -(value + damping[d]) if v == w else -value
                coef = jnp.where(var_of == w, value, coef)
            hi, lo = split(pat_ref[6 + f] * coef)
            if f < 4:
                k_tr[rows, ROWS * f : ROWS * (f + 1)] = hi
                k_tr[low_rows, ROWS * f : ROWS * (f + 1)] = lo
            else:
                k_loc[rows, ROWS * (f + 1) : ROWS * (f + 2)] = hi
                k_loc[low_rows, ROWS * (f + 1) : ROWS * (f + 2)] = lo

    lane = lax.broadcasted_iota(jnp.int32, (FACE, 128), 1)

    def product(matrix, hi_ref, lo_ref):
        first = jnp.dot(matrix[...], hi_ref[...], preferred_element_type=F32)
        second = jnp.dot(matrix[pl.ds(0, ROWS * NV), :], lo_ref[...], preferred_element_type=F32)
        return first[: ROWS * NV] + first[ROWS * NV :] + second

    def local_part(source, p):
        for i in range(2):
            n = 2 * p + i
            cols = slice(128 * i, 128 * (i + 1))
            for v in range(NV):
                hi, lo = split(source[v, n])
                x_hi[pl.ds(ROWS * v, ROWS), cols] = hi
                x_lo[pl.ds(ROWS * v, ROWS), cols] = lo
                near = source[v, n, pl.ds(0, FACE, stride=5), :]
                far = source[v, n, pl.ds(4, FACE, stride=5), :]
                ax[0, pl.ds(FACE * v, FACE), :] = jnp.where(lane == 127, far, pltpu.roll(near, 127, 1))
                ax[1, pl.ds(FACE * v, FACE), :] = jnp.where(
                    lane == 0, inflow_cols[v, n, pl.ds(0, FACE), :], pltpu.roll(far, 1, 1)
                )
            for f in range(2):
                hi, lo = split(ax[f])
                x_hi[pl.ds(ROWS * (NV + f), ROWS), cols] = hi
                x_lo[pl.ds(ROWS * (NV + f), ROWS), cols] = lo
        total = product(k_loc, x_hi, x_lo)
        r[p, 0] = total[:, :128]
        r[p, 1] = total[:, 128:]

    row = lax.broadcasted_iota(jnp.int32, (ROWS, 128), 0)
    sign = jnp.where(jnp.logical_and(row >= 2 * FACE, row < 3 * FACE), -1.0, 1.0)

    def trace_part(x, p):
        def put(f, i, value):
            hi, lo = split(value)
            t_hi[pl.ds(ROWS * f, ROWS), 128 * i : 128 * (i + 1)] = hi
            t_lo[pl.ds(ROWS * f, ROWS), 128 * i : 128 * (i + 1)] = lo

        def arrived(f):
            face_copy(x, p, f).wait_recv()
            for i in range(2):
                put(f, i, faces[x, p, f, i])

        def mirrored(f):
            for i in range(2):
                put(f, i, sign * stage[x, p, 5 - f, i])

        for f, edge in ((2, at_top), (3, at_bottom)):
            pl.when(jnp.logical_not(edge))(functools.partial(arrived, f))
            pl.when(edge)(functools.partial(mirrored, f))
        for f in range(2):
            arrived(f)
        total = product(k_tr, t_hi, t_lo)
        r[p, 0] = r[p, 0] + total[:, :128]
        r[p, 1] = r[p, 1] + total[:, 128:]

    def finish(source, p):
        def one(i, c):
            inst = i // 4
            n = 2 * p + inst
            start = pl.multiple_of(lax.rem(i, 4) * CHUNK, CHUNK)
            rows = pl.ds(start, CHUNK)
            scale = metric[rows, :]
            values = [
                scale * r[p, inst, pl.ds(pl.multiple_of(ROWS * v + start, CHUNK), CHUNK), :] + spec[v, n, rows, :]
                for v in range(NV)
            ]
            for v in range(NV):
                total = pre_ref[n, pl.ds(NV * v, 1), :] * values[0]
                for w in range(1, NV):
                    total = total + pre_ref[n, pl.ds(NV * v + w, 1), :] * values[w]
                u[v, n, rows, :] = source[v, n, rows, :] - total
            return c

        lax.fori_loop(0, 8, one, 0)

    def results(p):
        for i in range(2):
            n = 2 * p + i
            for v in range(NV):
                rows = pl.ds(0, NODES)
                new_ref[n, v] = u[v, n, rows, :]
                res_ref[n, v] = metric[rows, :] * r[p, i, pl.ds(ROWS * v, NODES), :] + spec[v, n, rows, :]

    def weight(offset, n, m):
        return jnp.where(ahead, coupling(4 * offset + n - m), coupling(-4 * offset + n - m)).astype(F32)

    def send_cross(p, v):
        def one(c, carry):
            rows = pl.ds(pl.multiple_of(c * 16, 16), 16)
            mine = [us[v, m, rows, :] for m in range(4)]
            theirs = [raw[v, m, rows, :] for m in range(4)]
            for q in range(2):
                for i in range(2):
                    n = 2 * p + i
                    total = weight(1 + q, n, 0) * mine[0]
                    for m in range(1, 4):
                        total = total + weight(1 + q, n, m) * mine[m]
                    for m in range(4):
                        total = total + weight(2 + q, n, m) * theirs[m]
                    cross_out[p, v, q, i, rows, :] = total
            return carry

        lax.fori_loop(0, 8, one, 0)
        cross_copy(p, v).start()

    def inner_sums(p, v):
        cross_copy(p, v).wait_recv()

        def one(c, carry):
            rows = pl.ds(pl.multiple_of(c * 16, 16), 16)
            mine = [us[v, m, rows, :] for m in range(4)]
            theirs = [raw[v, m, rows, :] for m in range(4)]
            for i in range(2):
                n = 2 * p + i
                out = cross_in[p, v, 1, i, rows, :]
                own = cross_in[p, v, 0, i, rows, :]
                for m in range(4):
                    out = out + weight(-1, n, m) * mine[m]
                    if n != m:
                        own = own + coupling(n - m) * mine[m]
                    own = own + weight(1, n, m) * theirs[m]
                edge_out[p, v, i, rows, :] = out
                spec[v, n, rows, :] = own
            return carry

        lax.fori_loop(0, 8, one, 0)
        edge_copy(p, v).start()

    def outer_sums(p, v):
        edge_copy(p, v).wait_recv()

        def one(c, carry):
            rows = pl.ds(pl.multiple_of(c * 16, 16), 16)
            mine = [us[v, m, rows, :] for m in range(4)]
            for i in range(2):
                n = 2 * p + i
                own = edge_in[p, v, i, rows, :]
                for m in range(4):
                    if n != m:
                        own = own + coupling(n - m) * mine[m]
                spec[v, n, rows, :] = own
            return carry

        lax.fori_loop(0, 8, one, 0)

    def sums(p, variables):
        @pl.when(inner)
        def _():
            for v in variables:
                inner_sums(p, v)

        @pl.when(outer)
        def _():
            for v in variables:
                outer_sums(p, v)

    for p in range(2):
        local_part(us, p)

    @pl.when(inner)
    def _():
        for v in range(NV):
            raw_copy(v).wait_recv()
            send_cross(0, v)
        for v in range(NV):
            send_cross(1, v)

    for p in range(2):
        trace_part(0, p)

    def advance(source, x, p):
        finish(source, p)
        extract(u, x + 1, p)
        send_faces(x + 1, p)
        local_part(u, p)

    sums(0, range(NV))
    advance(us, 0, 0)
    sums(1, (0, 1))
    trace_part(1, 0)
    advance(u, 1, 0)
    sums(1, (2, 3))
    trace_part(2, 0)
    advance(u, 2, 0)
    sums(1, (4,))
    advance(us, 0, 1)
    trace_part(3, 0)
    results(0)
    trace_part(1, 1)
    advance(u, 1, 1)
    trace_part(2, 1)
    advance(u, 2, 1)
    trace_part(3, 1)
    results(1)

    for x in range(PASSES + 1):
        for p in range(2):
            face_copy(x, p, 0).wait_send()
            face_copy(x, p, 1).wait_send()

            @pl.when(jnp.logical_not(at_bottom))
            def _(x=x, p=p):
                face_copy(x, p, 2).wait_send()

            @pl.when(jnp.logical_not(at_top))
            def _(x=x, p=p):
                face_copy(x, p, 3).wait_send()

    @pl.when(outer)
    def _():
        for v in range(NV):
            raw_copy(v).wait_send()

    @pl.when(inner)
    def _():
        for p in range(2):
            for v in range(NV):
                cross_copy(p, v).wait_send()
                edge_copy(p, v).wait_send()


def per_device(state, metric_scale, flux_jacobians, preconditioner, inflow):
    vmem = pl.BlockSpec(memory_space=pltpu.VMEM)
    smem = pl.BlockSpec(memory_space=pltpu.SMEM)
    block = (4, NV, NODES, 128)
    dma = pltpu.SemaphoreType.DMA
    exchanges = PASSES + 1
    new_state, residual = pl.pallas_call(
        kernel,
        name="pseudo_step",
        out_shape=(jax.ShapeDtypeStruct(block, F32), jax.ShapeDtypeStruct(block, F32)),
        in_specs=[vmem, vmem, smem, vmem, vmem, vmem],
        out_specs=(vmem, vmem),
        scratch_shapes=[
            pltpu.VMEM((NV, 4, ROWS, 128), F32),
            pltpu.VMEM((NV, 4, ROWS, 128), F32),
            pltpu.VMEM((NV, 4, ROWS, 128), F32),
            pltpu.VMEM((ROWS, 128), F32),
            pltpu.VMEM((NV, 4, 32, 128), F32),
            pltpu.VMEM((2 * NV * ROWS, 7 * ROWS), BF16),
            pltpu.VMEM((2 * NV * ROWS, 4 * ROWS), BF16),
            pltpu.VMEM((7 * ROWS, 256), BF16),
            pltpu.VMEM((7 * ROWS, 256), BF16),
            pltpu.VMEM((4 * ROWS, 256), BF16),
            pltpu.VMEM((4 * ROWS, 256), BF16),
            pltpu.VMEM((2, 2, NV * ROWS, 128), F32),
            pltpu.VMEM((2, ROWS, 128), F32),
            pltpu.VMEM((exchanges, 2, 4, 2, ROWS, 128), F32),
            pltpu.VMEM((exchanges, 2, 4, 2, ROWS, 128), F32),
            pltpu.VMEM((NV, 4, ROWS, 128), F32),
            pltpu.VMEM((2, NV, 2, 2, ROWS, 128), F32),
            pltpu.VMEM((2, NV, 2, 2, ROWS, 128), F32),
            pltpu.VMEM((2, NV, 2, ROWS, 128), F32),
            pltpu.VMEM((2, NV, 2, ROWS, 128), F32),
            dma((exchanges, 2, 4)),
            dma((exchanges, 2, 4)),
            dma((NV,)),
            dma((NV,)),
            dma((2, NV)),
            dma((2, NV)),
            dma((2, NV)),
            dma((2, NV)),
        ],
        compiler_params=pltpu.CompilerParams(
            collective_id=0, has_side_effects=True, vmem_limit_bytes=60 * 2**20
        ),
    )(
        state.reshape(block),
        metric_scale.reshape(NODES, 128),
        flux_jacobians,
        preconditioner.reshape(4, NV * NV, 128),
        inflow.reshape(4, NV, FACE),
        jnp.asarray(patterns()),
    )
    return new_state.reshape(state.shape), residual.reshape(state.shape)


def solution(mesh):
    in_specs = (
        P("tm", None, "elem", None, None),
        P("elem", None, None),
        P(),
        P("tm", None, None, "elem", None),
        P("tm", None, "elem", None),
    )
    out_specs = (P("tm", None, "elem", None, None), P("tm", None, "elem", None, None))
    return jax.shard_map(
        per_device, mesh=mesh, in_specs=in_specs, out_specs=out_specs, check_vma=False
    )
```

profile of v0, /device:TPU:224, one launch (start us, length us, event | category | flops | bytes accessed | tf_op | source)
XLA Modules:
  0.0 179.7 jit_solution(7120550488058655899)
XLA Ops:
  0.6 0.7 copy.25
  1.3 0.6 copy.15.inflow_ref
  1.9 1.3 copy.13.jac_ref
  3.2 0.8 copy.11
  4.1 0.6 copy.14.pre_ref
  4.7 1.5 copy.24
  6.2 2.5 %copy.23 = f32[4,5,1,125,128]{4,3,2,1,0:T(8,128)} copy(f32[4,5,1,125,128]{4,2,3,1,0:T(1,128)} %param.6) | data formatting | bytes 2560000
  8.7 164.8 %pseudo_step.1 = (f32[4,5,125,128]{3,2,1,0:T(8,128)}, f32[4,5,125,128]{3,2,1,0:T(8,128)}) custom-call(f32[4,5,125,128]{3,2,1,0:T(8,128)} %bitcast.12, f32[125,128]{1,0:T(8,128)} %bitcast.15, f32[3,5,5]{2,1,0:T(8,128)} %copy.13.jac_ref, f32[4,25,128]{2,1,0:T(8,128)} %copy.14.pre_ref, f32[4,5,25]{2,1,0:T(8,128)} %copy.15.inflow_ref, ...), custom_call_target="tpu_custom_call" | custom-call | tf_op jit(solution)/shard_map/pseudo_step/pallas_call | solution.py:460
  173.5 0.0 copy-start
  173.5 3.8 %copy.16 = f32[4,5,1,125,128]{4,2,3,1,0:T(1,128)} copy(f32[4,5,1,125,128]{4,3,1,0,2:T(8,128)} %bitcast.14) | data formatting | bytes 2560000
  177.3 0.0 copy-done
  177.3 2.4 %copy.17 = f32[4,5,1,125,128]{4,2,3,1,0:T(1,128)} copy(f32[4,5,1,125,128]{4,3,1,0,2:T(8,128)S(1)} %bitcast.13) | data formatting | bytes 2560000
Async XLA Ops:
  173.5 3.8 %copy-start = (f32[4,5,125,128]{3,2,1,0:T(8,128)S(1)}, f32[4,5,125,128]{3,2,1,0:T(8,128)}, u32[]{:S(2)}) copy-start(f32[4,5,125,128]{3,2,1,0:T(8,128)} %get-tuple-element.5) | copy-start | bytes 3840004
where the time goes:
time: 180 us
  Pallas kernels  165 us (92%)
  local copies, waits for them, and re-layouts  14.2 us (8%)
    pallas_call x1, Pallas kernels, per_device(): pl.pallas_call(kernel, name='pseudo_step', out_shape=(jax.ShapeDtypeStruc...  165 us
    unnamed x9, local copies, waits for them, and re-layouts  13 us

commit v1 on v0

v1 whole, which is shorter than its diff:
```python
import functools
import math

import jax
import jax.numpy as jnp
import numpy as np
from jax import lax
from jax.experimental import pallas as pl
from jax.experimental.pallas import tpu as pltpu
from jax.sharding import PartitionSpec as P

NI = 16
NV = 5
PR = 8
PASSES = 3
ROWS = 128
NODES = 125
FACE = 25
CHUNK = 32
GROUPS = ((0, 2), (2, 1), (3, 1))
WHOLE = 2
VIA = ((0, 1), (0, 1), (0, 1))
MESH = pl.DeviceIdType.MESH
F32 = jnp.float32
BF16 = jnp.bfloat16


def gll_derivative():
    points = np.array([-1.0, -math.sqrt(3.0 / 7.0), 0.0, math.sqrt(3.0 / 7.0), 1.0])
    legendre = (35.0 * points**4 - 30.0 * points**2 + 3.0) / 8.0
    identity = np.eye(5, dtype=bool)
    spacing = np.where(identity, 1.0, points[:, None] - points[None, :])
    matrix = legendre[:, None] / legendre[None, :] / spacing
    corner = np.array([-5.0, 0.0, 0.0, 0.0, 5.0])[None, :]
    return np.where(identity, corner, matrix)


def coupling(offset):
    if offset % NI == 0:
        return 0.0
    angle = math.pi * offset / NI
    return 0.5 * (1.0 - 2.0 * (offset % 2)) * math.cos(angle) / math.sin(angle)


def patterns():
    table = gll_derivative()
    node = np.arange(NODES)
    index = [node // 25, (node // 5) % 5, node % 5]
    out = np.zeros((12, ROWS, ROWS))
    for d in range(3):
        others = [index[o] for o in range(3) if o != d]
        same = np.ones((NODES, NODES), bool)
        for o in others:
            same &= o[:, None] == o[None, :]
        out[d, :NODES, :NODES] = np.where(same, table[index[d][:, None], index[d][None, :]], 0.0)
        high, low = index[d] == 4, index[d] == 0
        out[d, node, node] += np.where(high, -5.0, 0.0) + np.where(low, 5.0, 0.0)
        out[3 + d, node, node] = np.where(high | low, 5.0, 0.0)
        for side, face in enumerate((high, low)):
            dest = node[face]
            for v in range(NV):
                out[6 + 2 * d + side, dest, FACE * v + np.arange(FACE)] = 5.0
    return out.astype(np.float32)


def split(value):
    high = value.astype(BF16)
    low = (value - high.astype(F32)).astype(BF16)
    return high, low


def kernel(
    state_ref, metric_ref, jac_ref, pre_ref, inflow_ref, pat_ref, new_ref, res_ref,
    us, u, spec, res, metric, pre, inflow_cols, k_loc, k_tr, x_hi, x_lo, t_hi, t_lo, r, ax,
    stage, faces, passing, raw, near_in, far_in, cross_out, cross_in, edge_out, edge_in,
    face_s, face_r, via_s, via_r, on_s, raw_s, raw_r, near_s, near_r, far_s, far_r, cross_s, cross_r, edge_s, edge_r, in_s, out_s,
):
    t = lax.axis_index("tm")
    e = lax.axis_index("elem")
    inner = jnp.logical_or(t == 1, t == 2)
    outer = jnp.logical_not(inner)
    ahead = t < 2
    beside = jnp.where(inner, jnp.where(t == 1, 0, 3), jnp.where(t == 0, 1, 2))
    opposite = jnp.where(inner, 3 - t, t)
    at_top = lax.rem(e, PR) == PR // 2 - 1
    at_bottom = lax.rem(e, PR) == PR // 2
    following = lax.rem(e + PR, 64)
    preceding = lax.rem(e + 64 - PR, 64)
    above = lax.rem(e + 1, 64)
    below = lax.rem(e + 63, 64)

    core, x_of, in_half = lax.rem(e, 2), lax.rem(e // 8, 4), lax.rem(e, 32)
    y_of = lax.rem(e // 2, 4)

    def at(x, y):
        return jnp.logical_and(jnp.logical_and(x_of == x, y_of == y), core == 1)

    routes = ((at(0, 0), at(1, 0), at(3, 0), -16), (at(3, 3), at(2, 3), at(0, 3), 16))
    used = [f for f in range(4) if any(f in faces_of for faces_of in VIA)]

    barrier = pltpu.get_barrier_semaphore()
    for peer in (following, preceding, above, below):
        pl.semaphore_signal(barrier, inc=1, device_id=(t, peer), device_id_type=MESH)
    for step in (1, 2, 3):
        pl.semaphore_signal(barrier, inc=1, device_id=(lax.rem(t + step, 4), e), device_id_type=MESH)

    for f in used:
        @pl.when(routes[f][2])
        def _(f=f):
            relay = lax.rem(e + 64 - routes[f][3], 64)
            pl.semaphore_signal(barrier, inc=1, device_id=(t, relay), device_id_type=MESH)

    def remote(source, target, send, recv, peer_t, peer_e):
        return pltpu.make_async_remote_copy(
            src_ref=source, dst_ref=target, send_sem=send, recv_sem=recv,
            device_id=(peer_t, peer_e), device_id_type=MESH,
        )

    def members(g):
        return pl.ds(GROUPS[g][0], GROUPS[g][1])

    def face_copy(x, g, f):
        peer = (preceding, following, below, above)[f]
        part = (x, f, members(g))
        return remote(stage.at[part], faces.at[part], face_s.at[x, g, f], face_r.at[x, g, f], t, peer)

    def via_copy(x, g, f):
        peer = (following, preceding)[f % 2]
        part = (x, f, members(g))
        return remote(stage.at[part], passing.at[part], via_s.at[x, g, f], via_r.at[x, g, f], t, peer)

    def on_copy(x, g, f):
        part = (x, f, members(g))
        peer = lax.rem(e + 64 + routes[f][3], 64)
        return remote(passing.at[part], faces.at[part], on_s.at[x, g, f], face_r.at[x, g, f], t, peer)

    def sending(x, g, f, act):
        wall = (None, None, at_bottom, at_top)[f]
        straight = None if wall is None else jnp.logical_not(wall)
        if f in VIA[g]:
            first = routes[f][0]
            rest = jnp.logical_not(first)
            straight = rest if straight is None else jnp.logical_and(straight, rest)
            pl.when(first)(lambda: act(via_copy(x, g, f)))
        if straight is None:
            act(face_copy(x, g, f))
        else:
            pl.when(straight)(lambda: act(face_copy(x, g, f)))

    def pass_on(x, g):
        for f in VIA[g]:

            @pl.when(routes[f][1])
            def _(f=f):
                via_copy(x, g, f).wait_recv()
                on_copy(x, g, f).start()

    def raw_copy(v):
        return remote(us.at[v], raw.at[v], raw_s.at[v], raw_r.at[v], beside, e)

    def near_copy(v):
        return remote(us.at[v], near_in.at[v], near_s.at[v], near_r.at[v], opposite, e)

    def far_copy(v):
        return remote(us.at[v], far_in.at[v], far_s.at[v], far_r.at[v], lax.rem(t + 2, 4), e)

    def cross_copy(g, v):
        part = (v, members(g))
        return remote(cross_out.at[part], cross_in.at[part], cross_s.at[g, v], cross_r.at[g, v], opposite, e)

    def edge_copy(g, v):
        part = (v, members(g))
        return remote(edge_out.at[part], edge_in.at[part], edge_s.at[g, v], edge_r.at[g, v], beside, e)

    nodes = pl.ds(0, NODES)
    loads = [
        pltpu.make_async_copy(state_ref.at[n, v, :, 0, :], us.at[v, n, nodes, :], in_s.at[v, n])
        for n in range(4)
        for v in range(NV)
    ]
    loads.append(pltpu.make_async_copy(metric_ref.at[:, 0, :], metric.at[nodes, :], in_s.at[NV, 0]))
    for n in range(4):
        loads.append(pltpu.make_async_copy(pre_ref.at[n, :, 0, :], pre.at[n], in_s.at[NV + 1, n]))
    for load in loads:
        load.start()
    last = pl.ds(NODES, ROWS - NODES)
    tail = pl.ds(ROWS - 8, 8)
    metric[last, :] = jnp.zeros((3, 128), F32)
    for v in range(NV):
        for n in range(4):
            us[v, n, last, :] = jnp.zeros((3, 128), F32)
    ax[:, tail, :] = jnp.zeros((2, 8, 128), F32)

    def clear(n, c):
        for x in range(PASSES + 1):
            for f in range(4):
                stage[x, f, n, tail, :] = jnp.zeros((8, 128), F32)
        return c

    lax.fori_loop(0, 4, clear, 0)

    def extract(source, x, g):
        def one(i, c):
            n = GROUPS[g][0] + i
            for v in range(NV):
                rows = pl.ds(FACE * v, FACE)
                stage[x, 0, n, rows, :] = source[v, n, pl.ds(0, FACE), :]
                stage[x, 1, n, rows, :] = source[v, n, pl.ds(100, FACE), :]
                for k in range(5):
                    stage[x, 2, n, pl.ds(FACE * v + 5 * k, 5), :] = source[v, n, pl.ds(25 * k, 5), :]
                    stage[x, 3, n, pl.ds(FACE * v + 5 * k, 5), :] = source[v, n, pl.ds(25 * k + 20, 5), :]
            return c

        lax.fori_loop(0, GROUPS[g][1], one, 0)

    def send_faces(x, g):
        for f in (0, 1, 2, 3):
            sending(x, g, f, lambda copy: copy.start())

    for load in loads:
        load.wait()

    expected = 7
    for f in used:
        expected = expected + jnp.where(routes[f][1], 1, 0)
    pl.semaphore_wait(barrier, expected)

    @pl.when(outer)
    def _():
        order = []
        for v in range(WHOLE, NV):
            order.append(raw_copy(v))
            if v - WHOLE < WHOLE:
                order.append(far_copy(v - WHOLE))
        for v in range(NV - WHOLE, WHOLE):
            order.append(far_copy(v))
        for v in range(WHOLE):
            order.append(raw_copy(v))
        for copy in order:
            copy.start()

    @pl.when(inner)
    def _():
        for v in range(WHOLE):
            near_copy(v).start()

    for g in range(len(GROUPS)):
        extract(us, 0, g)
        send_faces(0, g)

    diagonal = lax.broadcasted_iota(jnp.int32, (FACE, FACE), 0) == lax.broadcasted_iota(
        jnp.int32, (FACE, FACE), 1
    )
    for n in range(4):
        for v in range(NV):
            row = inflow_ref[n, v]
            column = jnp.sum(jnp.where(diagonal, row, 0.0), axis=1, keepdims=True)
            inflow_cols[v, n, pl.ds(0, FACE), :] = jnp.broadcast_to(column, (FACE, 128))

    damping = []
    for d in range(3):
        sums = []
        for v in range(NV):
            total = jnp.abs(jac_ref[v, d, 0])
            for w in range(1, NV):
                total = total + jnp.abs(jac_ref[v, d, w])
            sums.append(total)
        largest = sums[0]
        for v in range(1, NV):
            largest = jnp.maximum(largest, sums[v])
        damping.append(largest)
    var_of = lax.broadcasted_iota(jnp.int32, (1, 128), 1) // FACE
    for v in range(NV):
        rows = pl.ds(ROWS * v, ROWS)
        low_rows = pl.ds(ROWS * (NV + v), ROWS)
        for w in range(NV):
            block = jac_ref[v, 0, w] * pat_ref[0]
            for d in range(1, 3):
                block = block + jac_ref[v, d, w] * pat_ref[d]
            if v == w:
                for d in range(3):
                    block = block + damping[d] * pat_ref[3 + d]
            hi, lo = split(block)
            k_loc[rows, ROWS * w : ROWS * (w + 1)] = hi
            k_loc[low_rows, ROWS * w : ROWS * (w + 1)] = lo
        for f in range(6):
            d, side = f // 2, f % 2
            coef = jnp.zeros((1, 128), F32)
            for w in range(NV):
                value = jac_ref[v, d, w]
                if side == 0:
                    value = value - damping[d] if v == w else value
                else:
                    value = -(value + damping[d]) if v == w else -value
                coef = jnp.where(var_of == w, value, coef)
            hi, lo = split(pat_ref[6 + f] * coef)
            if f < 4:
                k_tr[rows, ROWS * f : ROWS * (f + 1)] = hi
                k_tr[low_rows, ROWS * f : ROWS * (f + 1)] = lo
            else:
                k_loc[rows, ROWS * (f + 1) : ROWS * (f + 2)] = hi
                k_loc[low_rows, ROWS * (f + 1) : ROWS * (f + 2)] = lo

    lane = lax.broadcasted_iota(jnp.int32, (FACE, 128), 1)

    def product(matrix, hi, lo):
        first = jnp.dot(matrix[...], hi, preferred_element_type=F32)
        second = jnp.dot(matrix[pl.ds(0, ROWS * NV), :], lo, preferred_element_type=F32)
        return first[: ROWS * NV] + first[ROWS * NV :] + second

    def local_part(source, g):
        first, count = GROUPS[g]
        for i in range(count):
            n = first + i
            cols = slice(128 * i, 128 * (i + 1))
            for v in range(NV):
                hi, lo = split(source[v, n])
                x_hi[pl.ds(ROWS * v, ROWS), cols] = hi
                x_lo[pl.ds(ROWS * v, ROWS), cols] = lo
                near = source[v, n, pl.ds(0, FACE, stride=5), :]
                far = source[v, n, pl.ds(4, FACE, stride=5), :]
                ax[0, pl.ds(FACE * v, FACE), :] = jnp.where(lane == 127, far, pltpu.roll(near, 127, 1))
                ax[1, pl.ds(FACE * v, FACE), :] = jnp.where(
                    lane == 0, inflow_cols[v, n, pl.ds(0, FACE), :], pltpu.roll(far, 1, 1)
                )
            for f in range(2):
                hi, lo = split(ax[f])
                x_hi[pl.ds(ROWS * (NV + f), ROWS), cols] = hi
                x_lo[pl.ds(ROWS * (NV + f), ROWS), cols] = lo
        used = slice(0, 128 * count)
        total = product(k_loc, x_hi[:, used], x_lo[:, used])
        for i in range(count):
            r[first + i] = total[:, 128 * i : 128 * (i + 1)]

    row = lax.broadcasted_iota(jnp.int32, (ROWS, 128), 0)
    sign = jnp.where(jnp.logical_and(row >= 2 * FACE, row < 3 * FACE), -1.0, 1.0)

    def trace_part(x, g):
        first, count = GROUPS[g]

        def put(f, i, value):
            hi, lo = split(value)
            t_hi[pl.ds(ROWS * f, ROWS), 128 * i : 128 * (i + 1)] = hi
            t_lo[pl.ds(ROWS * f, ROWS), 128 * i : 128 * (i + 1)] = lo

        def arrived(f):
            face_copy(x, g, f).wait_recv()
            for i in range(count):
                put(f, i, faces[x, f, first + i])

        def mirrored(f):
            for i in range(count):
                put(f, i, sign * stage[x, 5 - f, first + i])

        for f, edge in ((2, at_top), (3, at_bottom)):
            pl.when(jnp.logical_not(edge))(functools.partial(arrived, f))
            pl.when(edge)(functools.partial(mirrored, f))
        for f in range(2):
            arrived(f)
        used = slice(0, 128 * count)
        total = product(k_tr, t_hi[:, used], t_lo[:, used])
        for i in range(count):
            r[first + i] = r[first + i] + total[:, 128 * i : 128 * (i + 1)]

    def finish(source, g):
        first, count = GROUPS[g]

        def one(i, c):
            n = first + i // 4
            start = pl.multiple_of(lax.rem(i, 4) * CHUNK, CHUNK)
            rows = pl.ds(start, CHUNK)
            scale = metric[rows, :]
            values = [
                scale * r[n, pl.ds(pl.multiple_of(ROWS * v + start, CHUNK), CHUNK), :] + spec[v, n, rows, :]
                for v in range(NV)
            ]
            for v in range(NV):
                total = pre[n, pl.ds(NV * v, 1), :] * values[0]
                for w in range(1, NV):
                    total = total + pre[n, pl.ds(NV * v + w, 1), :] * values[w]
                u[v, n, rows, :] = source[v, n, rows, :] - total
            return c

        lax.fori_loop(0, 4 * count, one, 0)

    def stores(g, kind):
        buffer, target = ((u, new_ref), (res, res_ref))[kind]
        first, count = GROUPS[g]
        return [
            pltpu.make_async_copy(buffer.at[v, n, nodes, :], target.at[n, v, :, 0, :], out_s.at[kind, v, n])
            for n in range(first, first + count)
            for v in range(NV)
        ]

    def results(g):
        first, count = GROUPS[g]
        for n in range(first, first + count):
            for v in range(NV):
                res[v, n] = metric[...] * r[n, pl.ds(ROWS * v, ROWS), :] + spec[v, n]
        for store in stores(g, 1):
            store.start()

    def weight(offset, n, m):
        return jnp.where(ahead, coupling(4 * offset + n - m), coupling(-4 * offset + n - m)).astype(F32)

    def tiles(body):
        def one(c, carry):
            body(pl.ds(pl.multiple_of(c * 16, 16), 16))
            return carry

        lax.fori_loop(0, 8, one, 0)

    def combine(total, offset, n, values):
        for m in range(4):
            total = total + weight(offset, n, m) * values[m]
        return total

    def own_part(total, n, values):
        for m in range(4):
            if n != m:
                total = total + coupling(n - m) * values[m]
        return total

    def instances(g):
        return range(GROUPS[g][0], GROUPS[g][0] + GROUPS[g][1])

    def send_cross(g, v):
        def body(rows):
            mine = [us[v, m, rows, :] for m in range(4)]
            theirs = [raw[v, m, rows, :] for m in range(4)]
            for n in instances(g):
                for q in range(2):
                    total = combine(jnp.zeros((16, 128), F32), 1 + q, n, mine)
                    cross_out[v, n, q, rows, :] = combine(total, 2 + q, n, theirs)

        tiles(body)
        cross_copy(g, v).start()

    def whole_sums(v):
        raw_copy(v).wait_recv()
        near_copy(v).wait_recv()
        far_copy(v).wait_recv()

        def body(rows):
            mine = [us[v, m, rows, :] for m in range(4)]
            theirs = [raw[v, m, rows, :] for m in range(4)]
            near = [near_in[v, m, rows, :] for m in range(4)]
            far = [far_in[v, m, rows, :] for m in range(4)]
            for n in range(4):
                zero = jnp.zeros((16, 128), F32)
                edge_out[v, n, rows, :] = combine(combine(combine(zero, -1, n, mine), -2, n, near), -3, n, far)
                spec[v, n, rows, :] = combine(
                    combine(combine(own_part(zero, n, mine), 1, n, theirs), -1, n, near), -2, n, far
                )

        tiles(body)
        edge_copy(0, v).start()

    def inner_sums(g, v):
        cross_copy(g, v).wait_recv()

        def body(rows):
            mine = [us[v, m, rows, :] for m in range(4)]
            theirs = [raw[v, m, rows, :] for m in range(4)]
            for n in instances(g):
                edge_out[v, n, rows, :] = combine(cross_in[v, n, 1, rows, :], -1, n, mine)
                spec[v, n, rows, :] = combine(own_part(cross_in[v, n, 0, rows, :], n, mine), 1, n, theirs)

        tiles(body)
        edge_copy(g, v).start()

    def outer_sums(g, v):
        edge_copy(g, v).wait_recv()

        def body(rows):
            mine = [us[v, m, rows, :] for m in range(4)]
            for n in instances(g):
                spec[v, n, rows, :] = own_part(edge_in[v, n, rows, :], n, mine)

        tiles(body)

    def sums(g):
        @pl.when(inner)
        def _():
            for v in range(WHOLE, NV):
                inner_sums(g, v)

        @pl.when(outer)
        def _():
            for v in range(NV):
                outer_sums(g, v)

    def advance(source, x, g):
        finish(source, g)
        extract(u, x + 1, g)
        send_faces(x + 1, g)
        if x == PASSES - 1:
            for store in stores(g, 0):
                store.start()
        local_part(u, g)
        pass_on(x + 1, g)

    for g in range(len(GROUPS)):
        local_part(us, g)
    for g in range(len(GROUPS)):
        pass_on(0, g)

    @pl.when(inner)
    def _():
        for v in range(WHOLE, NV):
            raw_copy(v).wait_recv()
            send_cross(0, v)
            if v > WHOLE:
                inner_sums(0, v - 1)
        for g in range(1, len(GROUPS)):
            for v in range(WHOLE, NV):
                send_cross(g, v)
        for v in range(WHOLE):
            whole_sums(v)
        inner_sums(0, NV - 1)
        for g in range(1, len(GROUPS)):
            for v in range(WHOLE):
                edge_copy(g, v).start()

    for g in range(len(GROUPS)):
        trace_part(0, g)

    @pl.when(outer)
    def _():
        for v in (*range(WHOLE, NV - 1), *range(WHOLE), NV - 1):
            outer_sums(0, v)

    advance(us, 0, 0)
    sums(1)
    advance(us, 0, 1)
    trace_part(1, 0)
    advance(u, 1, 0)
    sums(2)
    advance(us, 0, 2)
    trace_part(1, 1)
    advance(u, 1, 1)
    trace_part(2, 0)
    advance(u, 2, 0)
    trace_part(1, 2)
    advance(u, 1, 2)
    trace_part(2, 1)
    advance(u, 2, 1)
    trace_part(3, 0)
    results(0)
    trace_part(2, 2)
    advance(u, 2, 2)
    trace_part(3, 1)
    results(1)
    trace_part(3, 2)
    results(2)

    for g in range(len(GROUPS)):
        for kind in range(2):
            for store in stores(g, kind):
                store.wait()

    for g in range(len(GROUPS)):
        for x in range(PASSES + 1):
            for f in range(4):
                sending(x, g, f, lambda copy: copy.wait_send())
            for f in VIA[g]:

                @pl.when(routes[f][1])
                def _(x=x, g=g, f=f):
                    on_copy(x, g, f).wait_send()

    @pl.when(outer)
    def _():
        for v in range(NV):
            raw_copy(v).wait_send()
        for v in range(WHOLE):
            far_copy(v).wait_send()

    @pl.when(inner)
    def _():
        for v in range(WHOLE):
            near_copy(v).wait_send()
        for g in range(len(GROUPS)):
            for v in range(NV):
                if v >= WHOLE:
                    cross_copy(g, v).wait_send()
                edge_copy(g, v).wait_send()


def per_device(state, metric_scale, flux_jacobians, preconditioner, inflow):
    vmem = pl.BlockSpec(memory_space=pltpu.VMEM)
    smem = pl.BlockSpec(memory_space=pltpu.SMEM)
    block = (4, NV, NODES, 1, 128)
    hbm = pl.BlockSpec(memory_space=pl.ANY)
    dma = pltpu.SemaphoreType.DMA
    exchanges = PASSES + 1
    groups = len(GROUPS)
    new_state, residual = pl.pallas_call(
        kernel,
        name="pseudo_step",
        out_shape=(jax.ShapeDtypeStruct(block, F32), jax.ShapeDtypeStruct(block, F32)),
        in_specs=[hbm, hbm, smem, hbm, vmem, vmem],
        out_specs=(hbm, hbm),
        scratch_shapes=[
            pltpu.VMEM((NV, 4, ROWS, 128), F32),
            pltpu.VMEM((NV, 4, ROWS, 128), F32),
            pltpu.VMEM((NV, 4, ROWS, 128), F32),
            pltpu.VMEM((NV, 4, ROWS, 128), F32),
            pltpu.VMEM((ROWS, 128), F32),
            pltpu.VMEM((4, NV * NV, 128), F32),
            pltpu.VMEM((NV, 4, 32, 128), F32),
            pltpu.VMEM((2 * NV * ROWS, 7 * ROWS), BF16),
            pltpu.VMEM((2 * NV * ROWS, 4 * ROWS), BF16),
            pltpu.VMEM((7 * ROWS, 256), BF16),
            pltpu.VMEM((7 * ROWS, 256), BF16),
            pltpu.VMEM((4 * ROWS, 256), BF16),
            pltpu.VMEM((4 * ROWS, 256), BF16),
            pltpu.VMEM((4, NV * ROWS, 128), F32),
            pltpu.VMEM((2, ROWS, 128), F32),
            pltpu.VMEM((exchanges, 4, 4, ROWS, 128), F32),
            pltpu.VMEM((exchanges, 4, 4, ROWS, 128), F32),
            pltpu.VMEM((exchanges, 4, 4, ROWS, 128), F32),
            pltpu.VMEM((NV, 4, ROWS, 128), F32),
            pltpu.VMEM((WHOLE, 4, ROWS, 128), F32),
            pltpu.VMEM((WHOLE, 4, ROWS, 128), F32),
            pltpu.VMEM((NV, 4, 2, ROWS, 128), F32),
            pltpu.VMEM((NV, 4, 2, ROWS, 128), F32),
            pltpu.VMEM((NV, 4, ROWS, 128), F32),
            pltpu.VMEM((NV, 4, ROWS, 128), F32),
            dma((exchanges, groups, 4)),
            dma((exchanges, groups, 4)),
            dma((exchanges, groups, 4)),
            dma((exchanges, groups, 4)),
            dma((exchanges, groups, 4)),
            dma((NV,)),
            dma((NV,)),
            dma((WHOLE,)),
            dma((WHOLE,)),
            dma((WHOLE,)),
            dma((WHOLE,)),
            dma((groups, NV)),
            dma((groups, NV)),
            dma((groups, NV)),
            dma((groups, NV)),
            dma((NV + 2, 4)),
            dma((2, NV, 4)),
        ],
        compiler_params=pltpu.CompilerParams(
            collective_id=0, has_side_effects=True, vmem_limit_bytes=60 * 2**20
        ),
    )(
        state.reshape(block),
        metric_scale.reshape(NODES, 1, 128),
        flux_jacobians.transpose(1, 0, 2),
        preconditioner.reshape(4, NV * NV, 1, 128),
        inflow.reshape(4, NV, 1, FACE),
        jnp.asarray(patterns()),
    )
    return new_state.reshape(state.shape), residual.reshape(state.shape)


def solution(mesh):
    in_specs = (
        P("tm", None, "elem", None, None),
        P("elem", None, None),
        P(),
        P("tm", None, None, "elem", None),
        P("tm", None, "elem", None),
    )
    out_specs = (P("tm", None, "elem", None, None), P("tm", None, "elem", None, None))
    return jax.shard_map(
        per_device, mesh=mesh, in_specs=in_specs, out_specs=out_specs, check_vma=False
    )
```

time: 180 us -> 141 us (0.78)
  the two profiles are of different devices: /device:TPU:224 before, /device:TPU:25 now
where the time goes in v1:
time: 141 us
  Pallas kernels  136 us (96%)
  local copies, waits for them, and re-layouts  3.6 us (3%)
    pallas_call x1, Pallas kernels, per_device(): pl.pallas_call(kernel, name='pseudo_step', out_shape=(jax.ShapeDtypeStruc...  136 us
    unnamed x4, local copies, waits for them, and re-layouts  3.6 us

profile of v1, /device:TPU:25, one launch (start us, length us, event | category | flops | bytes accessed | tf_op | source)
XLA Modules:
  0.0 140.6 jit_solution(13017014827293147813)
XLA Ops:
  0.6 136.3 %pseudo_step.1 = (f32[4,5,125,1,128]{4,3,2,1,0:T(1,128)}, f32[4,5,125,1,128]{4,3,2,1,0:T(1,128)}) custom-call(f32[4,5,125,1,128]{4,3,2,1,0:T(1,128)} %bitcast.8, f32[125,1,128]{2,1,0:T(1,128)} %bitcast.9, f32[5,3,5]{2,1,0:T(4,128)} %bitcast.11, f32[4,25,1,128]{3,2,1,0:T(1,128)} %bitcast.10, f32[4,5,1,25]{3,2,1,0:T(1,128)} %inflow_ref.1, ...), custom_call_target="tpu_custom_call" | custom-call | tf_op jit(solution)/shard_map/pseudo_step/pallas_call | solution.py:598
  137.0 0.0 copy-start
  137.0 2.5 %copy.10 = f32[4,5,1,125,128]{4,2,3,1,0:T(1,128)} copy(f32[4,5,1,125,128]{4,2,3,1,0:T(1,128)} %bitcast.7) | data formatting | bytes 2560000
  139.5 0.0 copy-done
  139.5 1.0 copy.11
Async XLA Ops:
  137.0 2.6 %copy-start = (f32[4,5,125,1,128]{4,3,2,1,0:T(1,128)S(1)}, f32[4,5,125,1,128]{4,3,2,1,0:T(1,128)}, u32[]{:S(2)}) copy-start(f32[4,5,125,1,128]{4,3,2,1,0:T(1,128)} %get-tuple-element.5) | copy-start | bytes 3840004

commit v2 on v1

--- a/solution.py
+++ b/solution.py
@@ -19,7 +19,6 @@
 CHUNK = 32
 GROUPS = ((0, 2), (2, 1), (3, 1))
 WHOLE = 2
-VIA = ((0, 1), (0, 1), (0, 1))
 MESH = pl.DeviceIdType.MESH
 F32 = jnp.float32
 BF16 = jnp.bfloat16
@@ -89,14 +88,17 @@
     above = lax.rem(e + 1, 64)
     below = lax.rem(e + 63, 64)
 
-    core, x_of, in_half = lax.rem(e, 2), lax.rem(e // 8, 4), lax.rem(e, 32)
-    y_of = lax.rem(e // 2, 4)
-
-    def at(x, y):
-        return jnp.logical_and(jnp.logical_and(x_of == x, y_of == y), core == 1)
-
-    routes = ((at(0, 0), at(1, 0), at(3, 0), -16), (at(3, 3), at(2, 3), at(0, 3), 16))
-    used = [f for f in range(4) if any(f in faces_of for faces_of in VIA)]
+    core, x_of, y_of = lax.rem(e, 2), lax.rem(e // 8, 4), lax.rem(e // 2, 4)
+
+    def at(x):
+        return jnp.logical_and(x_of == x, core == 1)
+
+    def route(f, x):
+        edge, relay, other, distance, row = ((0, 1, 3, -16, 3), (3, 2, 0, 16, 0))[f]
+        places = [at(edge), at(relay), at(other)]
+        if x >= 2:
+            places = [jnp.logical_and(place, y_of != row) for place in places]
+        return (*places, distance)
 
     barrier = pltpu.get_barrier_semaphore()
     for peer in (following, preceding, above, below):
@@ -104,10 +106,12 @@
     for step in (1, 2, 3):
         pl.semaphore_signal(barrier, inc=1, device_id=(lax.rem(t + step, 4), e), device_id_type=MESH)
 
-    for f in used:
-        @pl.when(routes[f][2])
-        def _(f=f):
-            relay = lax.rem(e + 64 - routes[f][3], 64)
+    for f in range(2):
+        _, _, last_device, distance = route(f, 0)
+
+        @pl.when(last_device)
+        def _(distance=distance):
+            relay = lax.rem(e + 64 - distance, 64)
             pl.semaphore_signal(barrier, inc=1, device_id=(t, relay), device_id_type=MESH)
 
     def remote(source, target, send, recv, peer_t, peer_e):
@@ -131,14 +135,14 @@
 
     def on_copy(x, g, f):
         part = (x, f, members(g))
-        peer = lax.rem(e + 64 + routes[f][3], 64)
+        peer = lax.rem(e + 64 + route(f, x)[3], 64)
         return remote(passing.at[part], faces.at[part], on_s.at[x, g, f], face_r.at[x, g, f], t, peer)
 
     def sending(x, g, f, act):
         wall = (None, None, at_bottom, at_top)[f]
         straight = None if wall is None else jnp.logical_not(wall)
-        if f in VIA[g]:
-            first = routes[f][0]
+        if f < 2:
+            first = route(f, x)[0]
             rest = jnp.logical_not(first)
             straight = rest if straight is None else jnp.logical_and(straight, rest)
             pl.when(first)(lambda: act(via_copy(x, g, f)))
@@ -148,9 +152,9 @@
             pl.when(straight)(lambda: act(face_copy(x, g, f)))
 
     def pass_on(x, g):
-        for f in VIA[g]:
-
-            @pl.when(routes[f][1])
+        for f in range(2):
+
+            @pl.when(route(f, x)[1])
             def _(f=f):
                 via_copy(x, g, f).wait_recv()
                 on_copy(x, g, f).start()
@@ -221,8 +225,8 @@
         load.wait()
 
     expected = 7
-    for f in used:
-        expected = expected + jnp.where(routes[f][1], 1, 0)
+    for f in range(2):
+        expected = expected + jnp.where(route(f, 0)[1], 1, 0)
     pl.semaphore_wait(barrier, expected)
 
     @pl.when(outer)
@@ -498,7 +502,6 @@
             for store in stores(g, 0):
                 store.start()
         local_part(u, g)
-        pass_on(x + 1, g)
 
     for g in range(len(GROUPS)):
         local_part(us, g)
@@ -531,28 +534,22 @@
             outer_sums(0, v)
 
     advance(us, 0, 0)
-    sums(1)
-    advance(us, 0, 1)
-    trace_part(1, 0)
-    advance(u, 1, 0)
-    sums(2)
-    advance(us, 0, 2)
-    trace_part(1, 1)
-    advance(u, 1, 1)
-    trace_part(2, 0)
-    advance(u, 2, 0)
-    trace_part(1, 2)
-    advance(u, 1, 2)
-    trace_part(2, 1)
-    advance(u, 2, 1)
-    trace_part(3, 0)
-    results(0)
-    trace_part(2, 2)
-    advance(u, 2, 2)
-    trace_part(3, 1)
-    results(1)
-    trace_part(3, 2)
-    results(2)
+    for g in range(1, len(GROUPS)):
+        sums(g)
+        advance(us, 0, g)
+        pass_on(1, g - 1)
+    pass_on(1, len(GROUPS) - 1)
+    for x in range(1, PASSES + 1):
+        for g in range(len(GROUPS)):
+            trace_part(x, g)
+            if x == PASSES:
+                results(g)
+                continue
+            if g > 0:
+                pass_on(x + 1, g - 1)
+            advance(u, x, g)
+        if x < PASSES:
+            pass_on(x + 1, len(GROUPS) - 1)
 
     for g in range(len(GROUPS)):
         for kind in range(2):
@@ -563,9 +560,9 @@
         for x in range(PASSES + 1):
             for f in range(4):
                 sending(x, g, f, lambda copy: copy.wait_send())
-            for f in VIA[g]:
-
-                @pl.when(routes[f][1])
+            for f in range(2):
+
+                @pl.when(route(f, x)[1])
                 def _(x=x, g=g, f=f):
                     on_copy(x, g, f).wait_send()
 
@@ -598,9 +595,9 @@
     new_state, residual = pl.pallas_call(
         kernel,
         name="pseudo_step",
-        out_shape=(jax.ShapeDtypeStruct(block, F32), jax.ShapeDtypeStruct(block, F32)),
+        out_shape=(pltpu.VMEM(block, F32), pltpu.VMEM(block, F32)),
         in_specs=[hbm, hbm, smem, hbm, vmem, vmem],
-        out_specs=(hbm, hbm),
+        out_specs=(vmem, vmem),
         scratch_shapes=[
             pltpu.VMEM((NV, 4, ROWS, 128), F32),
             pltpu.VMEM((NV, 4, ROWS, 128), F32),

time: 141 us -> 134 us (0.950)
  Pallas kernels: 136 us -> 131 us
  local copies, waits for them, and re-layouts: 3.6 us -> 2.09 us
    pallas_call x1, Pallas kernels: 136 us -> 131 us  [per_device(): pl.pallas_call(kernel, name='pseudo_step', out_shape=(pltpu.VMEM(block, F...]
    unnamed x4 -> x2, local copies, waits for them, and re-layouts: 3.6 us -> 2.09 us
where the time goes in v2:
time: 134 us
  Pallas kernels  131 us (98%)
  local copies, waits for them, and re-layouts  2.09 us (2%)
    pallas_call x1, Pallas kernels, per_device(): pl.pallas_call(kernel, name='pseudo_step', out_shape=(pltpu.VMEM(block, F...  131 us

profile of v2, /device:TPU:25, one launch (start us, length us, event | category | flops | bytes accessed | tf_op | source)
XLA Modules:
  0.0 134.0 jit_solution(6249995631878491638)
XLA Ops:
  0.6 131.3 %pseudo_step.1 = (f32[4,5,125,1,128]{4,3,2,1,0:T(1,128)S(1)}, f32[4,5,125,1,128]{4,3,2,1,0:T(1,128)S(1)}) custom-call(f32[4,5,125,1,128]{4,3,2,1,0:T(1,128)} %bitcast.8, f32[125,1,128]{2,1,0:T(1,128)} %bitcast.9, f32[5,3,5]{2,1,0:T(4,128)} %bitcast.11, f32[4,25,1,128]{3,2,1,0:T(1,128)} %bitcast.10, f32[4,5,1,25]{3,2,1,0:T(1,128)} %inflow_ref.1, ...), custom_call_target="tpu_custom_call" | custom-call | tf_op jit(solution)/shard_map/pseudo_step/pallas_call | solution.py:595
  131.9 1.0 copy.10
  133.0 1.0 copy.11

commit v3 on v2

--- a/solution.py
+++ b/solution.py
@@ -17,7 +17,7 @@
 NODES = 125
 FACE = 25
 CHUNK = 32
-GROUPS = ((0, 2), (2, 1), (3, 1))
+INSTANCES = 4
 WHOLE = 2
 MESH = pl.DeviceIdType.MESH
 F32 = jnp.float32
@@ -96,14 +96,14 @@
     def route(f, x):
         edge, relay, other, distance, row = ((0, 1, 3, -16, 3), (3, 2, 0, 16, 0))[f]
         places = [at(edge), at(relay), at(other)]
-        if x >= 2:
-            places = [jnp.logical_and(place, y_of != row) for place in places]
+        relayed = jnp.logical_or(x < 2, y_of != row)
+        places = [jnp.logical_and(place, relayed) for place in places]
         return (*places, distance)
 
     barrier = pltpu.get_barrier_semaphore()
     for peer in (following, preceding, above, below):
         pl.semaphore_signal(barrier, inc=1, device_id=(t, peer), device_id_type=MESH)
-    for step in (1, 2, 3):
+    for step in (1, 3):
         pl.semaphore_signal(barrier, inc=1, device_id=(lax.rem(t + step, 4), e), device_id_type=MESH)
 
     for f in range(2):
@@ -120,21 +120,18 @@
             device_id=(peer_t, peer_e), device_id_type=MESH,
         )
 
-    def members(g):
-        return pl.ds(GROUPS[g][0], GROUPS[g][1])
-
     def face_copy(x, g, f):
         peer = (preceding, following, below, above)[f]
-        part = (x, f, members(g))
+        part = (x, f, g)
         return remote(stage.at[part], faces.at[part], face_s.at[x, g, f], face_r.at[x, g, f], t, peer)
 
     def via_copy(x, g, f):
         peer = (following, preceding)[f % 2]
-        part = (x, f, members(g))
+        part = (x, f, g)
         return remote(stage.at[part], passing.at[part], via_s.at[x, g, f], via_r.at[x, g, f], t, peer)
 
     def on_copy(x, g, f):
-        part = (x, f, members(g))
+        part = (x, f, g)
         peer = lax.rem(e + 64 + route(f, x)[3], 64)
         return remote(passing.at[part], faces.at[part], on_s.at[x, g, f], face_r.at[x, g, f], t, peer)
 
@@ -166,14 +163,14 @@
         return remote(us.at[v], near_in.at[v], near_s.at[v], near_r.at[v], opposite, e)
 
     def far_copy(v):
-        return remote(us.at[v], far_in.at[v], far_s.at[v], far_r.at[v], lax.rem(t + 2, 4), e)
+        return remote(raw.at[v], far_in.at[v], far_s.at[v], far_r.at[v], opposite, e)
 
     def cross_copy(g, v):
-        part = (v, members(g))
+        part = (v, g)
         return remote(cross_out.at[part], cross_in.at[part], cross_s.at[g, v], cross_r.at[g, v], opposite, e)
 
     def edge_copy(g, v):
-        part = (v, members(g))
+        part = (v, g)
         return remote(edge_out.at[part], edge_in.at[part], edge_s.at[g, v], edge_r.at[g, v], beside, e)
 
     nodes = pl.ds(0, NODES)
@@ -204,18 +201,13 @@
     lax.fori_loop(0, 4, clear, 0)
 
     def extract(source, x, g):
-        def one(i, c):
-            n = GROUPS[g][0] + i
-            for v in range(NV):
-                rows = pl.ds(FACE * v, FACE)
-                stage[x, 0, n, rows, :] = source[v, n, pl.ds(0, FACE), :]
-                stage[x, 1, n, rows, :] = source[v, n, pl.ds(100, FACE), :]
-                for k in range(5):
-                    stage[x, 2, n, pl.ds(FACE * v + 5 * k, 5), :] = source[v, n, pl.ds(25 * k, 5), :]
-                    stage[x, 3, n, pl.ds(FACE * v + 5 * k, 5), :] = source[v, n, pl.ds(25 * k + 20, 5), :]
-            return c
-
-        lax.fori_loop(0, GROUPS[g][1], one, 0)
+        for v in range(NV):
+            rows = pl.ds(FACE * v, FACE)
+            stage[x, 0, g, rows, :] = source[v, g, pl.ds(0, FACE), :]
+            stage[x, 1, g, rows, :] = source[v, g, pl.ds(100, FACE), :]
+            for k in range(5):
+                stage[x, 2, g, pl.ds(FACE * v + 5 * k, 5), :] = source[v, g, pl.ds(25 * k, 5), :]
+                stage[x, 3, g, pl.ds(FACE * v + 5 * k, 5), :] = source[v, g, pl.ds(25 * k + 20, 5), :]
 
     def send_faces(x, g):
         for f in (0, 1, 2, 3):
@@ -224,33 +216,33 @@
     for load in loads:
         load.wait()
 
-    expected = 7
+    expected = 6
     for f in range(2):
         expected = expected + jnp.where(route(f, 0)[1], 1, 0)
     pl.semaphore_wait(barrier, expected)
 
     @pl.when(outer)
     def _():
-        order = []
-        for v in range(WHOLE, NV):
-            order.append(raw_copy(v))
-            if v - WHOLE < WHOLE:
-                order.append(far_copy(v - WHOLE))
-        for v in range(NV - WHOLE, WHOLE):
-            order.append(far_copy(v))
-        for v in range(WHOLE):
-            order.append(raw_copy(v))
-        for copy in order:
-            copy.start()
+        for v in range(NV):
+            raw_copy(v).start()
 
     @pl.when(inner)
     def _():
         for v in range(WHOLE):
             near_copy(v).start()
 
-    for g in range(len(GROUPS)):
+    def each(body):
+        def one(g, c):
+            body(g)
+            return c
+
+        lax.fori_loop(0, INSTANCES, one, 0)
+
+    def begin(g):
         extract(us, 0, g)
         send_faces(0, g)
+
+    each(begin)
 
     diagonal = lax.broadcasted_iota(jnp.int32, (FACE, FACE), 0) == lax.broadcasted_iota(
         jnp.int32, (FACE, FACE), 1
@@ -313,65 +305,50 @@
         return first[: ROWS * NV] + first[ROWS * NV :] + second
 
     def local_part(source, g):
-        first, count = GROUPS[g]
-        for i in range(count):
-            n = first + i
-            cols = slice(128 * i, 128 * (i + 1))
-            for v in range(NV):
-                hi, lo = split(source[v, n])
-                x_hi[pl.ds(ROWS * v, ROWS), cols] = hi
-                x_lo[pl.ds(ROWS * v, ROWS), cols] = lo
-                near = source[v, n, pl.ds(0, FACE, stride=5), :]
-                far = source[v, n, pl.ds(4, FACE, stride=5), :]
-                ax[0, pl.ds(FACE * v, FACE), :] = jnp.where(lane == 127, far, pltpu.roll(near, 127, 1))
-                ax[1, pl.ds(FACE * v, FACE), :] = jnp.where(
-                    lane == 0, inflow_cols[v, n, pl.ds(0, FACE), :], pltpu.roll(far, 1, 1)
-                )
-            for f in range(2):
-                hi, lo = split(ax[f])
-                x_hi[pl.ds(ROWS * (NV + f), ROWS), cols] = hi
-                x_lo[pl.ds(ROWS * (NV + f), ROWS), cols] = lo
-        used = slice(0, 128 * count)
-        total = product(k_loc, x_hi[:, used], x_lo[:, used])
-        for i in range(count):
-            r[first + i] = total[:, 128 * i : 128 * (i + 1)]
+        for v in range(NV):
+            hi, lo = split(source[v, g])
+            x_hi[pl.ds(ROWS * v, ROWS), :] = hi
+            x_lo[pl.ds(ROWS * v, ROWS), :] = lo
+            near = source[v, g, pl.ds(0, FACE, stride=5), :]
+            far = source[v, g, pl.ds(4, FACE, stride=5), :]
+            ax[0, pl.ds(FACE * v, FACE), :] = jnp.where(lane == 127, far, pltpu.roll(near, 127, 1))
+            ax[1, pl.ds(FACE * v, FACE), :] = jnp.where(
+                lane == 0, inflow_cols[v, g, pl.ds(0, FACE), :], pltpu.roll(far, 1, 1)
+            )
+        for f in range(2):
+            hi, lo = split(ax[f])
+            x_hi[pl.ds(ROWS * (NV + f), ROWS), :] = hi
+            x_lo[pl.ds(ROWS * (NV + f), ROWS), :] = lo
+        r[g] = product(k_loc, x_hi[...], x_lo[...])
 
     row = lax.broadcasted_iota(jnp.int32, (ROWS, 128), 0)
     sign = jnp.where(jnp.logical_and(row >= 2 * FACE, row < 3 * FACE), -1.0, 1.0)
 
     def trace_part(x, g):
-        first, count = GROUPS[g]
-
-        def put(f, i, value):
+        def put(f, value):
             hi, lo = split(value)
-            t_hi[pl.ds(ROWS * f, ROWS), 128 * i : 128 * (i + 1)] = hi
-            t_lo[pl.ds(ROWS * f, ROWS), 128 * i : 128 * (i + 1)] = lo
+            t_hi[pl.ds(ROWS * f, ROWS), :] = hi
+            t_lo[pl.ds(ROWS * f, ROWS), :] = lo
 
         def arrived(f):
             face_copy(x, g, f).wait_recv()
-            for i in range(count):
-                put(f, i, faces[x, f, first + i])
+            put(f, faces[x, f, g])
 
         def mirrored(f):
-            for i in range(count):
-                put(f, i, sign * stage[x, 5 - f, first + i])
+            put(f, sign * stage[x, 5 - f, g])
 
         for f, edge in ((2, at_top), (3, at_bottom)):
             pl.when(jnp.logical_not(edge))(functools.partial(arrived, f))
             pl.when(edge)(functools.partial(mirrored, f))
         for f in range(2):
             arrived(f)
-        used = slice(0, 128 * count)
-        total = product(k_tr, t_hi[:, used], t_lo[:, used])
-        for i in range(count):
-            r[first + i] = r[first + i] + total[:, 128 * i : 128 * (i + 1)]
+        r[g] = r[g] + product(k_tr, t_hi[...], t_lo[...])
 
     def finish(source, g):
-        first, count = GROUPS[g]
+        n = g
 
         def one(i, c):
-            n = first + i // 4
-            start = pl.multiple_of(lax.rem(i, 4) * CHUNK, CHUNK)
+            start = pl.multiple_of(i * CHUNK, CHUNK)
             rows = pl.ds(start, CHUNK)
             scale = metric[rows, :]
             values = [
@@ -385,22 +362,18 @@
                 u[v, n, rows, :] = source[v, n, rows, :] - total
             return c
 
-        lax.fori_loop(0, 4 * count, one, 0)
+        lax.fori_loop(0, ROWS // CHUNK, one, 0)
 
     def stores(g, kind):
         buffer, target = ((u, new_ref), (res, res_ref))[kind]
-        first, count = GROUPS[g]
         return [
-            pltpu.make_async_copy(buffer.at[v, n, nodes, :], target.at[n, v, :, 0, :], out_s.at[kind, v, n])
-            for n in range(first, first + count)
+            pltpu.make_async_copy(buffer.at[v, g, nodes, :], target.at[g, v, :, 0, :], out_s.at[kind, v, g])
             for v in range(NV)
         ]
 
     def results(g):
-        first, count = GROUPS[g]
-        for n in range(first, first + count):
-            for v in range(NV):
-                res[v, n] = metric[...] * r[n, pl.ds(ROWS * v, ROWS), :] + spec[v, n]
+        for v in range(NV):
+            res[v, g] = metric[...] * r[g, pl.ds(ROWS * v, ROWS), :] + spec[v, g]
         for store in stores(g, 1):
             store.start()
 
@@ -425,14 +398,11 @@
                 total = total + coupling(n - m) * values[m]
         return total
 
-    def instances(g):
-        return range(GROUPS[g][0], GROUPS[g][0] + GROUPS[g][1])
-
     def send_cross(g, v):
         def body(rows):
             mine = [us[v, m, rows, :] for m in range(4)]
             theirs = [raw[v, m, rows, :] for m in range(4)]
-            for n in instances(g):
+            for n in (g,):
                 for q in range(2):
                     total = combine(jnp.zeros((16, 128), F32), 1 + q, n, mine)
                     cross_out[v, n, q, rows, :] = combine(total, 2 + q, n, theirs)
@@ -441,7 +411,6 @@
         cross_copy(g, v).start()
 
     def whole_sums(v):
-        raw_copy(v).wait_recv()
         near_copy(v).wait_recv()
         far_copy(v).wait_recv()
 
@@ -458,7 +427,8 @@
                 )
 
         tiles(body)
-        edge_copy(0, v).start()
+        for g in range(2):
+            edge_copy(g, v).start()
 
     def inner_sums(g, v):
         cross_copy(g, v).wait_recv()
@@ -466,7 +436,7 @@
         def body(rows):
             mine = [us[v, m, rows, :] for m in range(4)]
             theirs = [raw[v, m, rows, :] for m in range(4)]
-            for n in instances(g):
+            for n in (g,):
                 edge_out[v, n, rows, :] = combine(cross_in[v, n, 1, rows, :], -1, n, mine)
                 spec[v, n, rows, :] = combine(own_part(cross_in[v, n, 0, rows, :], n, mine), 1, n, theirs)
 
@@ -478,7 +448,7 @@
 
         def body(rows):
             mine = [us[v, m, rows, :] for m in range(4)]
-            for n in instances(g):
+            for n in (g,):
                 spec[v, n, rows, :] = own_part(edge_in[v, n, rows, :], n, mine)
 
         tiles(body)
@@ -486,7 +456,7 @@
     def sums(g):
         @pl.when(inner)
         def _():
-            for v in range(WHOLE, NV):
+            for v in range(WHOLE if g >= 2 else NV - 1, NV):
                 inner_sums(g, v)
 
         @pl.when(outer)
@@ -498,86 +468,102 @@
         finish(source, g)
         extract(u, x + 1, g)
         send_faces(x + 1, g)
-        if x == PASSES - 1:
+
+        @pl.when(x == PASSES - 1)
+        def _():
             for store in stores(g, 0):
                 store.start()
+
         local_part(u, g)
 
-    for g in range(len(GROUPS)):
-        local_part(us, g)
-    for g in range(len(GROUPS)):
-        pass_on(0, g)
+    each(lambda g: local_part(us, g))
+    each(lambda g: pass_on(0, g))
 
     @pl.when(inner)
     def _():
+        for v in range(WHOLE):
+            raw_copy(v).wait_recv()
+            far_copy(v).start()
         for v in range(WHOLE, NV):
             raw_copy(v).wait_recv()
-            send_cross(0, v)
-            if v > WHOLE:
-                inner_sums(0, v - 1)
-        for g in range(1, len(GROUPS)):
+            for g in range(2):
+                send_cross(g, v)
+            if v - WHOLE < WHOLE:
+                whole_sums(v - WHOLE)
+        for g in range(2, INSTANCES):
             for v in range(WHOLE, NV):
                 send_cross(g, v)
-        for v in range(WHOLE):
-            whole_sums(v)
-        inner_sums(0, NV - 1)
-        for g in range(1, len(GROUPS)):
-            for v in range(WHOLE):
-                edge_copy(g, v).start()
-
-    for g in range(len(GROUPS)):
-        trace_part(0, g)
-
-    @pl.when(outer)
-    def _():
-        for v in (*range(WHOLE, NV - 1), *range(WHOLE), NV - 1):
-            outer_sums(0, v)
-
-    advance(us, 0, 0)
-    for g in range(1, len(GROUPS)):
+        for v in range(WHOLE, NV - 1):
+            for g in range(2):
+                inner_sums(g, v)
+
+    each(lambda g: trace_part(0, g))
+
+    for g in range(INSTANCES):
         sums(g)
+        if g == 1:
+
+            @pl.when(inner)
+            def _():
+                for n in range(2, INSTANCES):
+                    for v in range(WHOLE):
+                        edge_copy(n, v).start()
+
         advance(us, 0, g)
-        pass_on(1, g - 1)
-    pass_on(1, len(GROUPS) - 1)
-    for x in range(1, PASSES + 1):
-        for g in range(len(GROUPS)):
-            trace_part(x, g)
-            if x == PASSES:
-                results(g)
-                continue
-            if g > 0:
-                pass_on(x + 1, g - 1)
-            advance(u, x, g)
-        if x < PASSES:
-            pass_on(x + 1, len(GROUPS) - 1)
-
-    for g in range(len(GROUPS)):
+        if g > 0:
+            pass_on(1, g - 1)
+    pass_on(1, INSTANCES - 1)
+
+    def middle(i, c):
+        x, g = 1 + i // INSTANCES, lax.rem(i, INSTANCES)
+        trace_part(x, g)
+
+        @pl.when(g > 0)
+        def _():
+            pass_on(x + 1, g - 1)
+
+        advance(u, x, g)
+
+        @pl.when(g == INSTANCES - 1)
+        def _():
+            pass_on(x + 1, g)
+
+        return c
+
+    lax.fori_loop(0, (PASSES - 1) * INSTANCES, middle, 0)
+
+    def end(g):
+        trace_part(PASSES, g)
+        results(g)
+
+    each(end)
+
+    def drain(g):
         for kind in range(2):
             for store in stores(g, kind):
                 store.wait()
-
-    for g in range(len(GROUPS)):
         for x in range(PASSES + 1):
             for f in range(4):
                 sending(x, g, f, lambda copy: copy.wait_send())
             for f in range(2):
 
                 @pl.when(route(f, x)[1])
-                def _(x=x, g=g, f=f):
+                def _(x=x, f=f):
                     on_copy(x, g, f).wait_send()
+
+    each(drain)
 
     @pl.when(outer)
     def _():
         for v in range(NV):
             raw_copy(v).wait_send()
-        for v in range(WHOLE):
-            far_copy(v).wait_send()
 
     @pl.when(inner)
     def _():
         for v in range(WHOLE):
             near_copy(v).wait_send()
-        for g in range(len(GROUPS)):
+            far_copy(v).wait_send()
+        for g in range(INSTANCES):
             for v in range(NV):
                 if v >= WHOLE:
                     cross_copy(g, v).wait_send()
@@ -591,7 +577,7 @@
     hbm = pl.BlockSpec(memory_space=pl.ANY)
     dma = pltpu.SemaphoreType.DMA
     exchanges = PASSES + 1
-    groups = len(GROUPS)
+    groups = INSTANCES
     new_state, residual = pl.pallas_call(
         kernel,
         name="pseudo_step",
@@ -608,10 +594,10 @@
             pltpu.VMEM((NV, 4, 32, 128), F32),
             pltpu.VMEM((2 * NV * ROWS, 7 * ROWS), BF16),
             pltpu.VMEM((2 * NV * ROWS, 4 * ROWS), BF16),
-            pltpu.VMEM((7 * ROWS, 256), BF16),
-            pltpu.VMEM((7 * ROWS, 256), BF16),
-            pltpu.VMEM((4 * ROWS, 256), BF16),
-            pltpu.VMEM((4 * ROWS, 256), BF16),
+            pltpu.VMEM((7 * ROWS, 128), BF16),
+            pltpu.VMEM((7 * ROWS, 128), BF16),
+            pltpu.VMEM((4 * ROWS, 128), BF16),
+            pltpu.VMEM((4 * ROWS, 128), BF16),
             pltpu.VMEM((4, NV * ROWS, 128), F32),
             pltpu.VMEM((2, ROWS, 128), F32),
             pltpu.VMEM((exchanges, 4, 4, ROWS, 128), F32),

time: 134 us -> 131 us (0.978)
  Pallas kernels: 131 us -> 128 us
    pallas_call x1, Pallas kernels: 131 us -> 128 us  [per_device(): pl.pallas_call(kernel, name='pseudo_step', out_shape=(pltpu.VMEM(block, F...]
where the time goes in v3:
time: 131 us; the launch traced here: 130 us
  Pallas kernels  128 us (98%)
  local copies, waits for them, and re-layouts  2.09 us (2%)
    pallas_call x1, Pallas kernels, per_device(): pl.pallas_call(kernel, name='pseudo_step', out_shape=(pltpu.VMEM(block, F...  128 us

profile of v3, /device:TPU:25, one launch (start us, length us, event | category | flops | bytes accessed | tf_op | source)
XLA Modules:
  0.0 130.3 jit_solution(17117053247425076392)
XLA Ops:
  0.6 127.6 %pseudo_step.1 = (f32[4,5,125,1,128]{4,3,2,1,0:T(1,128)S(1)}, f32[4,5,125,1,128]{4,3,2,1,0:T(1,128)S(1)}) custom-call(f32[4,5,125,1,128]{4,3,2,1,0:T(1,128)} %bitcast.8, f32[125,1,128]{2,1,0:T(1,128)} %bitcast.9, f32[5,3,5]{2,1,0:T(4,128)} %bitcast.11, f32[4,25,1,128]{3,2,1,0:T(1,128)} %bitcast.10, f32[4,5,1,25]{3,2,1,0:T(1,128)} %inflow_ref.1, ...), custom_call_target="tpu_custom_call" | custom-call | tf_op jit(solution)/shard_map/pseudo_step/pallas_call | solution.py:581
  128.2 1.0 copy.10
  129.3 1.0 copy.11

commit v4 on v3

--- a/solution.py
+++ b/solution.py
@@ -210,7 +210,7 @@
                 stage[x, 3, g, pl.ds(FACE * v + 5 * k, 5), :] = source[v, g, pl.ds(25 * k + 20, 5), :]
 
     def send_faces(x, g):
-        for f in (0, 1, 2, 3):
+        for f in (2, 3, 0, 1):
             sending(x, g, f, lambda copy: copy.start())
 
     for load in loads:

time: 131 us -> 130 us (level)
  Pallas kernels: 128 us -> 126 us
    pallas_call x1, Pallas kernels: 128 us -> 126 us  [per_device(): pl.pallas_call(kernel, name='pseudo_step', out_shape=(pltpu.VMEM(block, F...]
where the time goes in v4:
time: 130 us; the launch traced here: 129 us
  Pallas kernels  126 us (97%)
  local copies, waits for them, and re-layouts  2.09 us (2%)
    pallas_call x1, Pallas kernels, per_device(): pl.pallas_call(kernel, name='pseudo_step', out_shape=(pltpu.VMEM(block, F...  126 us

profile of v4, /device:TPU:25, one launch (start us, length us, event | category | flops | bytes accessed | tf_op | source)
XLA Modules:
  0.0 128.7 jit_solution(9746424546564233648)
XLA Ops:
  0.6 126.0 %pseudo_step.1 = (f32[4,5,125,1,128]{4,3,2,1,0:T(1,128)S(1)}, f32[4,5,125,1,128]{4,3,2,1,0:T(1,128)S(1)}) custom-call(f32[4,5,125,1,128]{4,3,2,1,0:T(1,128)} %bitcast.8, f32[125,1,128]{2,1,0:T(1,128)} %bitcast.9, f32[5,3,5]{2,1,0:T(4,128)} %bitcast.11, f32[4,25,1,128]{3,2,1,0:T(1,128)} %bitcast.10, f32[4,5,1,25]{3,2,1,0:T(1,128)} %inflow_ref.1, ...), custom_call_target="tpu_custom_call" | custom-call | tf_op jit(solution)/shard_map/pseudo_step/pallas_call | solution.py:581
  126.6 1.0 copy.10
  127.7 1.0 copy.11
